TPU v7x, 256 devices: a whole 4x4x8 slice. The times are simulated.
256 devices in a mesh: sub: 32 (over x, z), col: 8 (over y, core).
Axes of the slice: x: 4, y: 4, z: 8, core: 2. Of those that a mesh axis runs over, the one named last changes fastest.
Arguments:
- trace_start: bfloat16 [32, 8, 1536, 128], P('sub', 'col'), may hold values from -6 to 6
- neumann_load: bfloat16 [32, 8, 1536, 128], P('sub', 'col'), may hold values from -6 to 6
- double_layer: bfloat16 [32, 8, 1536, 1536], P('sub', 'col'), may hold values from -0.15625 to 0.15625
- single_inverse: bfloat16 [32, 8, 1536, 1536], P('sub', 'col'), may hold values from -0.15625 to 0.15625
- interface_nodes: int32 [32, 8, 8, 128], P('sub', 'col'), may hold values from -1 to 1023, as said below
- node_mode: int32 [32, 8, 1536], P('sub', 'col'), may hold values from 0 to 63
- mode_weight: bfloat16 [32, 8, 1536], P('sub', 'col'), may hold values from 0.5 to 1.5
- coarse_inverse: bfloat16 [16384, 16384], P('sub', 'col'), may hold values from -0.005859375 to 0.005859375
Outputs:
- final_trace: bfloat16 [32, 8, 1536, 128], P('sub', 'col')
- final_residual: bfloat16 [32, 8, 1536, 128], P('sub', 'col')
Inputs may be any that keep to these rules, and one draw needn't show every extreme that they name: `interface_nodes`: entry k of block (s, d) is a boundary node of s, within nodes d * 128 to (d + 1) * 128 - 1, distinct within the block, and matches entry k of the neighbour's block for direction 7 - d; valid entries come first and the rest are -1; blocks toward outside the grid are all -1; blocks of directions 1, 3, 4, 6 have 128 / 2 to 128 valid entries, the others 1 to 16, and some block has 128.
All inputs are finite; a program needn't handle non-finite values.
Results may differ from a plain program's by a relative error of at most 0.019.
Values may be sent and summed in bfloat16 or wider, within the bound.
A program may use at most 64 MiB of HBM per device.

v0:
```python
import jax
import jax.numpy as jnp
from jax import lax
from jax.sharding import PartitionSpec as P

MODES = 64
ITERS = 3
DIRECTIONS = ((-1, -1), (-1, 0), (-1, 1), (0, -1), (0, 1), (1, -1), (1, 0), (1, 1))


def from_behind(value, axis, by):
    devices = lax.axis_size(axis)
    pairs = [(i, i + by) for i in range(devices) if 0 <= i + by < devices]
    return lax.ppermute(value, axis, pairs)


def deliver_single(outgoing):
    arrivals = []
    for toward in range(8):
        row_step, col_step = DIRECTIONS[toward]
        message = outgoing[7 - toward]
        if row_step != 0:
            message = from_behind(message, "sub", -row_step)
        if col_step != 0:
            message = from_behind(message, "col", -col_step)
        arrivals.append(message)
    return jnp.stack(arrivals)


def local(
    trace_start,
    neumann_load,
    double_layer,
    single_inverse,
    interface_nodes,
    node_mode,
    mode_weight,
    coarse_inverse,
):
    trace_now = trace_start[0, 0]
    load_block = neumann_load[0, 0].astype(jnp.float32)
    kernel = double_layer[0, 0]
    inverse = single_inverse[0, 0]
    node_count = kernel.shape[0]
    interface = interface_nodes[0, 0]
    slot_count = interface.shape[1]
    band_rows = 8 * slot_count
    local_index = interface - (jnp.arange(8, dtype=jnp.int32) * slot_count)[:, None]
    selector = (
        local_index[:, :, None] == jnp.arange(slot_count, dtype=jnp.int32)[None, None, :]
    ).astype(jnp.bfloat16)
    mode_basis = jnp.where(
        node_mode[0, 0][None, :] == jnp.arange(MODES, dtype=jnp.int32)[:, None],
        mode_weight[0, 0][None, :],
        jnp.zeros((), jnp.bfloat16),
    )
    rhs_count = trace_now.shape[1]
    residual = trace_now
    rest_zeros = jnp.zeros((node_count - band_rows, rhs_count), jnp.float32)
    for iteration in range(ITERS):
        mixed_trace = (
            0.5 * trace_now.astype(jnp.float32)
            + jnp.dot(kernel, trace_now, preferred_element_type=jnp.float32)
        ).astype(jnp.bfloat16)
        flux_now = jnp.dot(inverse, mixed_trace, preferred_element_type=jnp.float32).astype(
            jnp.bfloat16
        )
        banded = flux_now[:band_rows].reshape(8, slot_count, rhs_count)
        outgoing = jnp.einsum(
            "dpq,dqr->dpr", selector, banded, preferred_element_type=jnp.float32
        ).astype(jnp.bfloat16)
        received = deliver_single(outgoing)
        placed = jnp.einsum(
            "dpq,dpr->dqr", selector, received, preferred_element_type=jnp.float32
        ).reshape(band_rows, rhs_count)
        assembled = flux_now.astype(jnp.float32) + jnp.concatenate([placed, rest_zeros], axis=0)
        residual = (load_block - assembled).astype(jnp.bfloat16)
        residual = lax.optimization_barrier(residual)
        coarse_rhs = jnp.dot(mode_basis, residual, preferred_element_type=jnp.float32).astype(
            jnp.bfloat16
        )
        partial_value = jnp.dot(
            coarse_inverse,
            lax.all_gather(coarse_rhs, "sub", axis=0, tiled=True),
            preferred_element_type=jnp.float32,
        )
        coarse_out = lax.psum_scatter(
            partial_value.astype(jnp.bfloat16), "col", scatter_dimension=0, tiled=True
        )
        correction = lax.dot_general(
            mode_basis, coarse_out, (((0,), (0,)), ((), ())), preferred_element_type=jnp.float32
        )
        trace_now = (
            trace_now.astype(jnp.float32) + 0.25 * residual.astype(jnp.float32) + correction
        ).astype(jnp.bfloat16)
    return (trace_now[None, None], residual[None, None])


def solution(mesh):
    placed = (
        P("sub", "col", None, None),
        P("sub", "col", None, None),
        P("sub", "col", None, None),
        P("sub", "col", None, None),
        P("sub", "col", None, None),
        P("sub", "col", None),
        P("sub", "col", None),
        P("sub", "col"),
    )
    return jax.shard_map(
        local,
        mesh=mesh,
        in_specs=placed,
        out_specs=(P("sub", "col", None, None), P("sub", "col", None, None)),
        check_vma=False,
    )
```

profile of v0, /device:TPU:2, one launch (start us, length us, event | category | flops | bytes accessed | tf_op | source)
XLA Modules:
  0.0 430.3 jit_solution(12199868396667985276)
XLA Ops:
  8.6 7.1 %fusion.54 = bf16[1536,128]{0,1:T(8,128)(2,1)S(1)} fusion(bf16[1,1,1536,1536]{3,2,1,0:T(8,128)(2,1)} %param.11, bf16[1,1,1536,1536]{3,2,1,0:T(8,128)(2,1)} %param.10, bf16[1,1,1536,128]{3,2,1,0:T(8,128)(2,1)} %param.8, bf16[1,1,1536,128]{2,3,1,0:T(8,128)(2,1)S(1)} %copy.26), kind=kOutput, calls=%fused_computation.31 | convolution fusion | flops 1208942592 | bytes 10616832 | tf_op jit(solution)/shard_map/dot_general | solution.py:65
  16.3 3.8 collective-permute-start
  20.2 5.9 %collective-permute-done = bf16[128,128]{1,0:T(8,128)(2,1)} collective-permute-done((bf16[128,128]{1,0:T(8,128)(2,1)S(1)}, bf16[128,128]{1,0:T(8,128)(2,1)}, u32[]{:S(2)}, u32[]{:S(2)}) %collective-permute-start) | collective-permute-done | bytes 32800 | tf_op jit(solution)/shard_map/ppermute | solution.py:14
  27.9 3.9 collective-permute-start.10
  56.2 3.8 collective-permute-start.8
  66.3 47.7 %all_gather.9 = bf16[2048,128]{1,0:T(8,128)(2,1)S(1)} all-gather(bf16[64,128]{1,0:T(8,128)(2,1)S(1)} %convolution_convert_fusion.8), channel_id=1, replica_groups=mesh['sub'=32,'col'=8] {'sub'}, dimensions={0}, use_global_device_ids=true | all-gather | bytes 540672 | tf_op jit(solution)/shard_map/all_gather | solution.py:84
  115.7 33.5 %reduce-scatter.10.cloned.1.call-done = bf16[64,128]{1,0:T(8,128)(2,1)} async-done(((bf16[512,128]{1,0:T(8,128)(2,1)}), bf16[64,128]{1,0:T(8,128)(2,1)}) %reduce-scatter.10.cloned.1.call-update) | async-done | bytes 16400
  150.5 6.9 %fusion.51 = bf16[1536,128]{0,1:T(8,128)(2,1)S(1)} fusion(bf16[1,1,1536,1536]{3,2,1,0:T(8,128)(2,1)} %param.11, bf16[1536,128]{0,1:T(8,128)(2,1)S(1)} %fusion.27, bf16[1,1,1536,1536]{3,2,1,0:T(8,128)(2,1)} %param.10), kind=kOutput, calls=%fused_computation.30 | convolution fusion | flops 1208942592 | bytes 10223616 | tf_op jit(solution)/shard_map/dot_general | solution.py:65
  159.7 3.5 collective-permute-start.12
  163.2 4.4 %collective-permute-done.12 = bf16[128,128]{1,0:T(8,128)(2,1)S(1)} collective-permute-done((bf16[128,128]{1,0:T(8,128)(2,1)S(1)}, bf16[128,128]{1,0:T(8,128)(2,1)S(1)}, u32[]{:S(2)}, u32[]{:S(2)}) %collective-permute-start.12) | collective-permute-done | bytes 32800 | tf_op jit(solution)/shard_map/ppermute | solution.py:14
  168.9 3.1 collective-permute-start.22
  172.0 3.3 collective-permute-start.21
  175.3 3.3 collective-permute-start.19
  194.7 3.8 collective-permute-start.20
  204.7 47.6 %all_gather.10 = bf16[2048,128]{1,0:T(8,128)(2,1)S(1)} all-gather(bf16[64,128]{1,0:T(8,128)(2,1)S(1)} %convolution_convert_fusion.7), channel_id=1, replica_groups=mesh['sub'=32,'col'=8] {'sub'}, dimensions={0}, use_global_device_ids=true | all-gather | bytes 540672 | tf_op jit(solution)/shard_map/all_gather | solution.py:84
  254.1 31.7 %reduce-scatter.12.cloned.1.call-done = bf16[64,128]{1,0:T(8,128)(2,1)} async-done(((bf16[512,128]{1,0:T(8,128)(2,1)}), bf16[64,128]{1,0:T(8,128)(2,1)}) %reduce-scatter.12.cloned.1.call-update) | async-done | bytes 16400
  287.1 6.9 %fusion.48 = bf16[1536,128]{0,1:T(8,128)(2,1)S(1)} fusion(bf16[1,1,1536,1536]{3,2,1,0:T(8,128)(2,1)} %param.11, bf16[1536,128]{0,1:T(8,128)(2,1)S(1)} %fusion.28, bf16[1,1,1536,1536]{3,2,1,0:T(8,128)(2,1)} %param.10), kind=kOutput, calls=%fused_computation.29 | convolution fusion | flops 1208942592 | bytes 10223616 | tf_op jit(solution)/shard_map/dot_general | solution.py:65
  296.4 3.5 collective-permute-start.24
  299.8 4.5 %collective-permute-done.24 = bf16[128,128]{1,0:T(8,128)(2,1)S(1)} collective-permute-done((bf16[128,128]{1,0:T(8,128)(2,1)S(1)}, bf16[128,128]{1,0:T(8,128)(2,1)S(1)}, u32[]{:S(2)}, u32[]{:S(2)}) %collective-permute-start.24) | collective-permute-done | bytes 32800 | tf_op jit(solution)/shard_map/ppermute | solution.py:14
  308.6 3.4 collective-permute-start.33
  312.0 3.2 collective-permute-start.31
  331.4 3.8 collective-permute-start.32
  340.7 47.7 %all_gather.11 = bf16[2048,128]{1,0:T(8,128)(2,1)S(1)} all-gather(bf16[64,128]{1,0:T(8,128)(2,1)S(1)} %convolution_convert_fusion.6), channel_id=1, replica_groups=mesh['sub'=32,'col'=8] {'sub'}, dimensions={0}, use_global_device_ids=true | all-gather | bytes 540672 | tf_op jit(solution)/shard_map/all_gather | solution.py:84
  390.9 31.0 %reduce-scatter.14.cloned.1.call-done = bf16[64,128]{1,0:T(8,128)(2,1)} async-done(((bf16[512,128]{1,0:T(8,128)(2,1)}), bf16[64,128]{1,0:T(8,128)(2,1)}) %reduce-scatter.14.cloned.1.call-update) | async-done | bytes 16400
  (140 shorter events, 98.6 us)
Async XLA Ops:
  7.2 142.0 %reduce-scatter.10.cloned.1.call-start = ((), (), s32[]{:S(2)}) async-start(), calls=%async_computation.3 | async-start | bytes 147456
  16.3 9.7 %collective-permute-start = (bf16[128,128]{1,0:T(8,128)(2,1)S(1)}, bf16[128,128]{1,0:T(8,128)(2,1)}, u32[]{:S(2)}, u32[]{:S(2)}) collective-permute-start(bf16[128,128]{1,0:T(8,128)(2,1)S(1)} %get-tuple-element.29), channel_id=1, source_target_pairs={{0,8},{8,16},{16,24},{24,32},{32,40},{40,48},{48,56},{56,64},{64,7... | collective-permute-start | bytes 98312 | tf_op jit(solution)/shard_map/ppermute | solution.py:14
  26.1 16.5 %collective-permute-start.1 = (bf16[128,128]{1,0:T(8,128)(2,1)}, bf16[128,128]{1,0:T(8,128)(2,1)}, u32[]{:S(2)}, u32[]{:S(2)}) collective-permute-start(bf16[128,128]{1,0:T(8,128)(2,1)} %collective-permute-done), channel_id=1, source_target_pairs={{0,1},{1,2},{2,3},{3,4},{4,5},{5,6},{6,7},{8,9},{9,10},{10,11},{11... | collective-permute-start | bytes 98312 | tf_op jit(solution)/shard_map/ppermute | solution.py:14
  27.9 23.9 %collective-permute-start.10 = (bf16[128,128]{1,0:T(8,128)(2,1)S(1)}, bf16[128,128]{1,0:T(8,128)(2,1)}, u32[]{:S(2)}, u32[]{:S(2)}) collective-permute-start(bf16[128,128]{1,0:T(8,128)(2,1)S(1)} %get-tuple-element.22), channel_id=1, source_target_pairs={{8,0},{16,8},{24,16},{32,24},{40,32},{48,40},{56,48},{64,56},{72,6... | collective-permute-start | bytes 98312 | tf_op jit(solution)/shard_map/ppermute | solution.py:14
  31.8 29.2 %collective-permute-start.9 = (bf16[128,128]{1,0:T(8,128)(2,1)S(1)}, bf16[128,128]{1,0:T(8,128)(2,1)S(1)}, u32[]{:S(2)}, u32[]{:S(2)}) collective-permute-start(bf16[128,128]{1,0:T(8,128)(2,1)S(1)} %get-tuple-element.23), channel_id=1, source_target_pairs={{8,0},{16,8},{24,16},{32,24},{40,32},{48,40},{56,48},{64,56},{72,6... | collective-permute-start | bytes 98312 | tf_op jit(solution)/shard_map/ppermute | solution.py:14
  34.8 20.1 %collective-permute-start.7 = (bf16[128,128]{1,0:T(8,128)(2,1)S(1)}, bf16[128,128]{1,0:T(8,128)(2,1)}, u32[]{:S(2)}, u32[]{:S(2)}) collective-permute-start(bf16[128,128]{1,0:T(8,128)(2,1)S(1)} %get-tuple-element.24), channel_id=1, source_target_pairs={{8,0},{16,8},{24,16},{32,24},{40,32},{48,40},{56,48},{64,56},{72,6... | collective-permute-start | bytes 98312 | tf_op jit(solution)/shard_map/ppermute | solution.py:14
  37.7 8.6 %collective-permute-start.3 = (bf16[128,128]{1,0:T(8,128)(2,1)S(1)}, bf16[128,128]{1,0:T(8,128)(2,1)}, u32[]{:S(2)}, u32[]{:S(2)}) collective-permute-start(bf16[128,128]{1,0:T(8,128)(2,1)S(1)} %get-tuple-element.27), channel_id=1, source_target_pairs={{0,8},{8,16},{16,24},{24,32},{32,40},{40,48},{48,56},{56,64},{64,7... | collective-permute-start | bytes 98312 | tf_op jit(solution)/shard_map/ppermute | solution.py:14
  46.3 13.7 %collective-permute-start.6 = (bf16[128,128]{1,0:T(8,128)(2,1)S(1)}, bf16[128,128]{1,0:T(8,128)(2,1)S(1)}, u32[]{:S(2)}, u32[]{:S(2)}) collective-permute-start(bf16[128,128]{1,0:T(8,128)(2,1)S(1)} %get-tuple-element.25), channel_id=1, source_target_pairs={{1,0},{2,1},{3,2},{4,3},{5,4},{6,5},{7,6},{9,8},{10,9},{11,10},{12... | collective-permute-start | bytes 98312 | tf_op jit(solution)/shard_map/ppermute | solution.py:14
  51.8 8.2 %collective-permute-start.5 = (bf16[128,128]{1,0:T(8,128)(2,1)S(1)}, bf16[128,128]{1,0:T(8,128)(2,1)S(1)}, u32[]{:S(2)}, u32[]{:S(2)}) collective-permute-start(bf16[128,128]{1,0:T(8,128)(2,1)S(1)} %get-tuple-element.26), channel_id=1, source_target_pairs={{0,1},{1,2},{2,3},{3,4},{4,5},{5,6},{6,7},{8,9},{9,10},{10,11},{11... | collective-permute-start | bytes 98312 | tf_op jit(solution)/shard_map/ppermute | solution.py:14
  115.6 170.2 %reduce-scatter.12.cloned.1.call-start = ((), (), s32[]{:S(2)}) async-start(), calls=%async_computation.4 | async-start | bytes 147456
  167.6 13.5 %collective-permute-start.13 = (bf16[128,128]{1,0:T(8,128)(2,1)S(1)}, bf16[128,128]{1,0:T(8,128)(2,1)S(1)}, u32[]{:S(2)}, u32[]{:S(2)}) collective-permute-start(bf16[128,128]{1,0:T(8,128)(2,1)S(1)} %collective-permute-done.12), channel_id=1, source_target_pairs={{0,1},{1,2},{2,3},{3,4},{4,5},{5,6},{6,7},{8,9},{9,10},{10,11},{11... | collective-permute-start | bytes 98312 | tf_op jit(solution)/shard_map/ppermute | solution.py:14
  168.9 21.5 %collective-permute-start.22 = (bf16[128,128]{1,0:T(8,128)(2,1)S(1)}, bf16[128,128]{1,0:T(8,128)(2,1)S(1)}, u32[]{:S(2)}, u32[]{:S(2)}) collective-permute-start(bf16[128,128]{1,0:T(8,128)(2,1)S(1)} %get-tuple-element.14), channel_id=1, source_target_pairs={{8,0},{16,8},{24,16},{32,24},{40,32},{48,40},{56,48},{64,56},{72,6... | collective-permute-start | bytes 98312 | tf_op jit(solution)/shard_map/ppermute | solution.py:14
  172.0 27.4 %collective-permute-start.21 = (bf16[128,128]{1,0:T(8,128)(2,1)S(1)}, bf16[128,128]{1,0:T(8,128)(2,1)S(1)}, u32[]{:S(2)}, u32[]{:S(2)}) collective-permute-start(bf16[128,128]{1,0:T(8,128)(2,1)S(1)} %get-tuple-element.15), channel_id=1, source_target_pairs={{8,0},{16,8},{24,16},{32,24},{40,32},{48,40},{56,48},{64,56},{72,6... | collective-permute-start | bytes 98312 | tf_op jit(solution)/shard_map/ppermute | solution.py:14
  175.3 18.1 %collective-permute-start.19 = (bf16[128,128]{1,0:T(8,128)(2,1)S(1)}, bf16[128,128]{1,0:T(8,128)(2,1)S(1)}, u32[]{:S(2)}, u32[]{:S(2)}) collective-permute-start(bf16[128,128]{1,0:T(8,128)(2,1)S(1)} %get-tuple-element.16), channel_id=1, source_target_pairs={{8,0},{16,8},{24,16},{32,24},{40,32},{48,40},{56,48},{64,56},{72,6... | collective-permute-start | bytes 98312 | tf_op jit(solution)/shard_map/ppermute | solution.py:14
  186.6 11.9 %collective-permute-start.18 = (bf16[128,128]{1,0:T(8,128)(2,1)S(1)}, bf16[128,128]{1,0:T(8,128)(2,1)S(1)}, u32[]{:S(2)}, u32[]{:S(2)}) collective-permute-start(bf16[128,128]{1,0:T(8,128)(2,1)S(1)} %get-tuple-element.17), channel_id=1, source_target_pairs={{1,0},{2,1},{3,2},{4,3},{5,4},{6,5},{7,6},{9,8},{10,9},{11,10},{12... | collective-permute-start | bytes 98312 | tf_op jit(solution)/shard_map/ppermute | solution.py:14
  190.4 8.2 %collective-permute-start.17 = (bf16[128,128]{1,0:T(8,128)(2,1)S(1)}, bf16[128,128]{1,0:T(8,128)(2,1)S(1)}, u32[]{:S(2)}, u32[]{:S(2)}) collective-permute-start(bf16[128,128]{1,0:T(8,128)(2,1)S(1)} %get-tuple-element.18), channel_id=1, source_target_pairs={{0,1},{1,2},{2,3},{3,4},{4,5},{5,6},{6,7},{8,9},{9,10},{10,11},{11... | collective-permute-start | bytes 98312 | tf_op jit(solution)/shard_map/ppermute | solution.py:14
  253.9 168.0 %reduce-scatter.14.cloned.1.call-start = ((), (), s32[]{:S(2)}) async-start(), calls=%async_computation.5 | async-start | bytes 147456
  304.3 13.5 %collective-permute-start.25 = (bf16[128,128]{1,0:T(8,128)(2,1)S(1)}, bf16[128,128]{1,0:T(8,128)(2,1)S(1)}, u32[]{:S(2)}, u32[]{:S(2)}) collective-permute-start(bf16[128,128]{1,0:T(8,128)(2,1)S(1)} %collective-permute-done.24), channel_id=1, source_target_pairs={{0,1},{1,2},{2,3},{3,4},{4,5},{5,6},{6,7},{8,9},{9,10},{10,11},{11... | collective-permute-start | bytes 98312 | tf_op jit(solution)/shard_map/ppermute | solution.py:14
  305.6 21.5 %collective-permute-start.34 = (bf16[128,128]{1,0:T(8,128)(2,1)S(1)}, bf16[128,128]{1,0:T(8,128)(2,1)S(1)}, u32[]{:S(2)}, u32[]{:S(2)}) collective-permute-start(bf16[128,128]{1,0:T(8,128)(2,1)S(1)} %get-tuple-element.6), channel_id=1, source_target_pairs={{8,0},{16,8},{24,16},{32,24},{40,32},{48,40},{56,48},{64,56},{72,6... | collective-permute-start | bytes 98312 | tf_op jit(solution)/shard_map/ppermute | solution.py:14
  308.6 27.5 %collective-permute-start.33 = (bf16[128,128]{1,0:T(8,128)(2,1)S(1)}, bf16[128,128]{1,0:T(8,128)(2,1)S(1)}, u32[]{:S(2)}, u32[]{:S(2)}) collective-permute-start(bf16[128,128]{1,0:T(8,128)(2,1)S(1)} %get-tuple-element.7), channel_id=1, source_target_pairs={{8,0},{16,8},{24,16},{32,24},{40,32},{48,40},{56,48},{64,56},{72,6... | collective-permute-start | bytes 98312 | tf_op jit(solution)/shard_map/ppermute | solution.py:14
  312.0 18.1 %collective-permute-start.31 = (bf16[128,128]{1,0:T(8,128)(2,1)S(1)}, bf16[128,128]{1,0:T(8,128)(2,1)S(1)}, u32[]{:S(2)}, u32[]{:S(2)}) collective-permute-start(bf16[128,128]{1,0:T(8,128)(2,1)S(1)} %get-tuple-element.8), channel_id=1, source_target_pairs={{8,0},{16,8},{24,16},{32,24},{40,32},{48,40},{56,48},{64,56},{72,6... | collective-permute-start | bytes 98312 | tf_op jit(solution)/shard_map/ppermute | solution.py:14
  315.2 8.1 %collective-permute-start.27 = (bf16[128,128]{1,0:T(8,128)(2,1)S(1)}, bf16[128,128]{1,0:T(8,128)(2,1)S(1)}, u32[]{:S(2)}, u32[]{:S(2)}) collective-permute-start(bf16[128,128]{1,0:T(8,128)(2,1)S(1)} %get-tuple-element.11), channel_id=1, source_target_pairs={{0,8},{8,16},{16,24},{24,32},{32,40},{40,48},{48,56},{56,64},{64,7... | collective-permute-start | bytes 98312 | tf_op jit(solution)/shard_map/ppermute | solution.py:14
  323.3 11.9 %collective-permute-start.30 = (bf16[128,128]{1,0:T(8,128)(2,1)S(1)}, bf16[128,128]{1,0:T(8,128)(2,1)S(1)}, u32[]{:S(2)}, u32[]{:S(2)}) collective-permute-start(bf16[128,128]{1,0:T(8,128)(2,1)S(1)} %get-tuple-element.9), channel_id=1, source_target_pairs={{1,0},{2,1},{3,2},{4,3},{5,4},{6,5},{7,6},{9,8},{10,9},{11,10},{12... | collective-permute-start | bytes 98312 | tf_op jit(solution)/shard_map/ppermute | solution.py:14
  327.1 8.2 %collective-permute-start.29 = (bf16[128,128]{1,0:T(8,128)(2,1)S(1)}, bf16[128,128]{1,0:T(8,128)(2,1)S(1)}, u32[]{:S(2)}, u32[]{:S(2)}) collective-permute-start(bf16[128,128]{1,0:T(8,128)(2,1)S(1)} %get-tuple-element.10), channel_id=1, source_target_pairs={{0,1},{1,2},{2,3},{3,4},{4,5},{5,6},{6,7},{8,9},{9,10},{10,11},{11... | collective-permute-start | bytes 98312 | tf_op jit(solution)/shard_map/ppermute | solution.py:14
  (21 other events, 288.8 us)
Sparse Core Ops, SparseCore 0:
  115.8 33.4 reduce-scatter.9
  254.0 31.7 reduce-scatter.11
  390.1 31.7 reduce-scatter.13
where the time goes:
time: 432 us; the launch traced here: 430 us
  blocking collectives  143 us (33%)
  waiting for transfers between devices  125 us (29%)
  starting transfers between devices  92.6 us (21%)
  matrix products  31.9 us (7%)
  local copies, waits for them, and re-layouts  19.3 us (4%)
  between operations  14.6 us (3%)
  other arithmetic  4.39 us (1%)
    all_gather x3, blocking collectives, local(): lax.all_gather(coarse_rhs, 'sub', axis=0, tiled=True)  143 us
    unnamed x6, waiting for transfers between devices  96.2 us
    ppermute x36, starting transfers between devices, from_behind(): return lax.ppermute(value, axis, pairs)  92.3 us
    ppermute x36, waiting for transfers between devices, from_behind(): return lax.ppermute(value, axis, pairs)  28.5 us
    dot_general x3, matrix products, local(): jnp.dot(inverse, mixed_trace, preferred_element_type=jnp.float32)  21 us
    unnamed x40, local copies, waits for them, and re-layouts  9.05 us
  transfers between devices with their start and end apart: 39, of which 14 were waited for; matrix products, arithmetic and copies ran while one was open for 1% of the time, Pallas kernels for 0%

commit v1 on v0

--- a/solution.py
+++ b/solution.py
@@ -6,6 +6,11 @@
 MODES = 64
 ITERS = 3
 DIRECTIONS = ((-1, -1), (-1, 0), (-1, 1), (0, -1), (0, 1), (1, -1), (1, 0), (1, 1))
+
+
+def gather_by_exchange(x, axis, dim):
+    copies = jnp.concatenate([x] * lax.axis_size(axis), axis=dim)
+    return lax.all_to_all(copies, axis, dim, dim, tiled=True)
 
 
 def from_behind(value, axis, by):
@@ -81,7 +86,7 @@
         )
         partial_value = jnp.dot(
             coarse_inverse,
-            lax.all_gather(coarse_rhs, "sub", axis=0, tiled=True),
+            gather_by_exchange(coarse_rhs, "sub", 0),
             preferred_element_type=jnp.float32,
         )
         coarse_out = lax.psum_scatter(

time: 432 us -> 352 us (0.81)
  blocking collectives: 143 us -> 61.5 us
    all_gather x3 -> x0, blocking collectives: 143 us -> none  [local(): lax.all_gather(coarse_rhs, 'sub', axis=0, tiled=True)]
    all_to_all x0 -> x3, blocking collectives: none -> 61.5 us  [gather_by_exchange(): return lax.all_to_all(copies, axis, dim, dim, tiled=True)]
    unnamed x40 -> x130, local copies, waits for them, and re-layouts: 9.05 us -> 8.57 us
where the time goes in v1:
time: 352 us; the launch traced here: 350 us
  waiting for transfers between devices  126 us (36%)
  starting transfers between devices  92.8 us (26%)
  blocking collectives  61.5 us (17%)
  matrix products  31.8 us (9%)
  local copies, waits for them, and re-layouts  18.9 us (5%)
  between operations  14.9 us (4%)
  other arithmetic  4.39 us (1%)
    unnamed x6, waiting for transfers between devices  97.6 us
    ppermute x36, starting transfers between devices, from_behind(): return lax.ppermute(value, axis, pairs)  92.5 us
    all_to_all x3, blocking collectives, gather_by_exchange(): return lax.all_to_all(copies, axis, dim, dim, tiled=True)  61.5 us
    ppermute x36, waiting for transfers between devices, from_behind(): return lax.ppermute(value, axis, pairs)  28.3 us
    dot_general x3, matrix products, local(): jnp.dot(inverse, mixed_trace, preferred_element_type=jnp.float32)  21 us
    unnamed x130, local copies, waits for them, and re-layouts  8.57 us
  transfers between devices with their start and end apart: 39, of which 14 were waited for; matrix products, arithmetic and copies ran while one was open for 1% of the time, Pallas kernels for 0%

profile of v1, /device:TPU:2, one launch (start us, length us, event | category | flops | bytes accessed | tf_op | source)
XLA Modules:
  0.0 350.2 jit_solution(17364207616822793384)
XLA Ops:
  8.6 7.1 %fusion.54 = bf16[1536,128]{0,1:T(8,128)(2,1)S(1)} fusion(bf16[1,1,1536,1536]{3,2,1,0:T(8,128)(2,1)} %param.11, bf16[1,1,1536,1536]{3,2,1,0:T(8,128)(2,1)} %param.10, bf16[1,1,1536,128]{3,2,1,0:T(8,128)(2,1)} %param.8, bf16[1,1,1536,128]{2,3,1,0:T(8,128)(2,1)S(1)} %copy.26), kind=kOutput, calls=%fused_computation.31 | convolution fusion | flops 1208942592 | bytes 10616832 | tf_op jit(solution)/shard_map/dot_general | solution.py:70
  16.3 3.8 %collective-permute-start = (bf16[128,128]{1,0:T(8,128)(2,1)S(1)}, bf16[128,128]{1,0:T(8,128)(2,1)}, u32[]{:S(2)}, u32[]{:S(2)}) collective-permute-start(bf16[128,128]{1,0:T(8,128)(2,1)S(1)} %get-tuple-element.29), channel_id=1, source_target_pairs={{0,8},{8,16},{16,24},{24,32},{32,40},{40,48},{48,56},{56,64},{64,7... | collective-permute-start | bytes 98312 | tf_op jit(solution)/shard_map/ppermute | solution.py:19
  20.2 5.9 %collective-permute-done = bf16[128,128]{1,0:T(8,128)(2,1)} collective-permute-done((bf16[128,128]{1,0:T(8,128)(2,1)S(1)}, bf16[128,128]{1,0:T(8,128)(2,1)}, u32[]{:S(2)}, u32[]{:S(2)}) %collective-permute-start) | collective-permute-done | bytes 32800 | tf_op jit(solution)/shard_map/ppermute | solution.py:19
  27.9 3.9 %collective-permute-start.10 = (bf16[128,128]{1,0:T(8,128)(2,1)S(1)}, bf16[128,128]{1,0:T(8,128)(2,1)}, u32[]{:S(2)}, u32[]{:S(2)}) collective-permute-start(bf16[128,128]{1,0:T(8,128)(2,1)S(1)} %get-tuple-element.22), channel_id=1, source_target_pairs={{8,0},{16,8},{24,16},{32,24},{40,32},{48,40},{56,48},{64,56},{72,6... | collective-permute-start | bytes 98312 | tf_op jit(solution)/shard_map/ppermute | solution.py:19
  56.2 3.8 %collective-permute-start.8 = (bf16[128,128]{1,0:T(8,128)(2,1)}, bf16[128,128]{1,0:T(8,128)(2,1)S(1)}, u32[]{:S(2)}, u32[]{:S(2)}) collective-permute-start(bf16[128,128]{1,0:T(8,128)(2,1)} %collective-permute-done.7), channel_id=1, source_target_pairs={{0,1},{1,2},{2,3},{3,4},{4,5},{5,6},{6,7},{8,9},{9,10},{10,11},{11... | collective-permute-start | bytes 98312 | tf_op jit(solution)/shard_map/ppermute | solution.py:19
  66.1 20.7 %all_to_all.36 = bf16[32,64,128]{2,1,0:T(8,128)(2,1)S(1)} all-to-all(bf16[32,64,128]{2,1,0:T(8,128)(2,1)S(1)} %bitcast.237), channel_id=1, replica_groups=mesh['sub'=32,'col'=8] {'sub'}, dimensions={0} | all-to-all | bytes 1048576 | tf_op jit(solution)/shard_map/all_to_all | solution.py:13
  88.5 34.7 %reduce-scatter.10.cloned.1.call-done = bf16[64,128]{1,0:T(8,128)(2,1)} async-done(((bf16[512,128]{1,0:T(8,128)(2,1)}), bf16[64,128]{1,0:T(8,128)(2,1)}) %reduce-scatter.10.cloned.1.call-update) | async-done | bytes 16400
  124.5 6.9 %fusion.51 = bf16[1536,128]{0,1:T(8,128)(2,1)S(1)} fusion(bf16[1,1,1536,1536]{3,2,1,0:T(8,128)(2,1)} %param.11, bf16[1536,128]{0,1:T(8,128)(2,1)S(1)} %fusion.27, bf16[1,1,1536,1536]{3,2,1,0:T(8,128)(2,1)} %param.10), kind=kOutput, calls=%fused_computation.30 | convolution fusion | flops 1208942592 | bytes 10223616 | tf_op jit(solution)/shard_map/dot_general | solution.py:70
  133.7 3.5 collective-permute-start.12
  137.1 4.5 %collective-permute-done.12 = bf16[128,128]{1,0:T(8,128)(2,1)S(1)} collective-permute-done((bf16[128,128]{1,0:T(8,128)(2,1)S(1)}, bf16[128,128]{1,0:T(8,128)(2,1)S(1)}, u32[]{:S(2)}, u32[]{:S(2)}) %collective-permute-start.12) | collective-permute-done | bytes 32800 | tf_op jit(solution)/shard_map/ppermute | solution.py:19
  146.0 3.3 collective-permute-start.21
  149.3 3.3 collective-permute-start.19
  168.8 3.8 %collective-permute-start.20 = (bf16[128,128]{1,0:T(8,128)(2,1)S(1)}, bf16[128,128]{1,0:T(8,128)(2,1)S(1)}, u32[]{:S(2)}, u32[]{:S(2)}) collective-permute-start(bf16[128,128]{1,0:T(8,128)(2,1)S(1)} %collective-permute-done.19), channel_id=1, source_target_pairs={{0,1},{1,2},{2,3},{3,4},{4,5},{5,6},{6,7},{8,9},{9,10},{10,11},{11... | collective-permute-start | bytes 98312 | tf_op jit(solution)/shard_map/ppermute | solution.py:19
  178.4 20.4 %all_to_all.37 = bf16[32,64,128]{2,1,0:T(8,128)(2,1)S(1)} all-to-all(bf16[32,64,128]{2,1,0:T(8,128)(2,1)S(1)} %bitcast.238), channel_id=1, replica_groups=mesh['sub'=32,'col'=8] {'sub'}, dimensions={0} | all-to-all | bytes 1048576 | tf_op jit(solution)/shard_map/all_to_all | solution.py:13
  200.6 31.7 %reduce-scatter.12.cloned.1.call-done = bf16[64,128]{1,0:T(8,128)(2,1)} async-done(((bf16[512,128]{1,0:T(8,128)(2,1)}), bf16[64,128]{1,0:T(8,128)(2,1)}) %reduce-scatter.12.cloned.1.call-update) | async-done | bytes 16400
  233.6 6.9 %fusion.48 = bf16[1536,128]{0,1:T(8,128)(2,1)S(1)} fusion(bf16[1,1,1536,1536]{3,2,1,0:T(8,128)(2,1)} %param.11, bf16[1536,128]{0,1:T(8,128)(2,1)S(1)} %fusion.28, bf16[1,1,1536,1536]{3,2,1,0:T(8,128)(2,1)} %param.10), kind=kOutput, calls=%fused_computation.29 | convolution fusion | flops 1208942592 | bytes 10223616 | tf_op jit(solution)/shard_map/dot_general | solution.py:70
  242.9 3.6 %collective-permute-start.24 = (bf16[128,128]{1,0:T(8,128)(2,1)S(1)}, bf16[128,128]{1,0:T(8,128)(2,1)S(1)}, u32[]{:S(2)}, u32[]{:S(2)}) collective-permute-start(bf16[128,128]{1,0:T(8,128)(2,1)S(1)} %get-tuple-element.13), channel_id=1, source_target_pairs={{0,8},{8,16},{16,24},{24,32},{32,40},{40,48},{48,56},{56,64},{64,7... | collective-permute-start | bytes 98312 | tf_op jit(solution)/shard_map/ppermute | solution.py:19
  246.4 4.4 %collective-permute-done.24 = bf16[128,128]{1,0:T(8,128)(2,1)S(1)} collective-permute-done((bf16[128,128]{1,0:T(8,128)(2,1)S(1)}, bf16[128,128]{1,0:T(8,128)(2,1)S(1)}, u32[]{:S(2)}, u32[]{:S(2)}) %collective-permute-start.24) | collective-permute-done | bytes 32800 | tf_op jit(solution)/shard_map/ppermute | solution.py:19
  252.1 3.2 collective-permute-start.34
  255.3 3.2 collective-permute-start.33
  258.5 3.3 collective-permute-start.31
  278.0 3.8 %collective-permute-start.32 = (bf16[128,128]{1,0:T(8,128)(2,1)S(1)}, bf16[128,128]{1,0:T(8,128)(2,1)S(1)}, u32[]{:S(2)}, u32[]{:S(2)}) collective-permute-start(bf16[128,128]{1,0:T(8,128)(2,1)S(1)} %collective-permute-done.31), channel_id=1, source_target_pairs={{0,1},{1,2},{2,3},{3,4},{4,5},{5,6},{6,7},{8,9},{9,10},{10,11},{11... | collective-permute-start | bytes 98312 | tf_op jit(solution)/shard_map/ppermute | solution.py:19
  287.7 20.4 %all_to_all.38 = bf16[32,64,128]{2,1,0:T(8,128)(2,1)S(1)} all-to-all(bf16[32,64,128]{2,1,0:T(8,128)(2,1)S(1)} %bitcast.239), channel_id=1, replica_groups=mesh['sub'=32,'col'=8] {'sub'}, dimensions={0} | all-to-all | bytes 1048576 | tf_op jit(solution)/shard_map/all_to_all | solution.py:13
  310.6 31.1 %reduce-scatter.14.cloned.1.call-done = bf16[64,128]{1,0:T(8,128)(2,1)} async-done(((bf16[512,128]{1,0:T(8,128)(2,1)}), bf16[64,128]{1,0:T(8,128)(2,1)}) %reduce-scatter.14.cloned.1.call-update) | async-done | bytes 16400
  (233 shorter events, 98.2 us)
Async XLA Ops:
  7.2 116.0 %reduce-scatter.10.cloned.1.call-start = ((), (), s32[]{:S(2)}) async-start(), calls=%async_computation.6 | async-start | bytes 147456
  16.3 9.7 %collective-permute-start = (bf16[128,128]{1,0:T(8,128)(2,1)S(1)}, bf16[128,128]{1,0:T(8,128)(2,1)}, u32[]{:S(2)}, u32[]{:S(2)}) collective-permute-start(bf16[128,128]{1,0:T(8,128)(2,1)S(1)} %get-tuple-element.29), channel_id=1, source_target_pairs={{0,8},{8,16},{16,24},{24,32},{32,40},{40,48},{48,56},{56,64},{64,7... | collective-permute-start | bytes 98312 | tf_op jit(solution)/shard_map/ppermute | solution.py:19
  26.1 16.5 %collective-permute-start.1 = (bf16[128,128]{1,0:T(8,128)(2,1)}, bf16[128,128]{1,0:T(8,128)(2,1)}, u32[]{:S(2)}, u32[]{:S(2)}) collective-permute-start(bf16[128,128]{1,0:T(8,128)(2,1)} %collective-permute-done), channel_id=1, source_target_pairs={{0,1},{1,2},{2,3},{3,4},{4,5},{5,6},{6,7},{8,9},{9,10},{10,11},{11... | collective-permute-start | bytes 98312 | tf_op jit(solution)/shard_map/ppermute | solution.py:19
  27.9 23.9 %collective-permute-start.10 = (bf16[128,128]{1,0:T(8,128)(2,1)S(1)}, bf16[128,128]{1,0:T(8,128)(2,1)}, u32[]{:S(2)}, u32[]{:S(2)}) collective-permute-start(bf16[128,128]{1,0:T(8,128)(2,1)S(1)} %get-tuple-element.22), channel_id=1, source_target_pairs={{8,0},{16,8},{24,16},{32,24},{40,32},{48,40},{56,48},{64,56},{72,6... | collective-permute-start | bytes 98312 | tf_op jit(solution)/shard_map/ppermute | solution.py:19
  31.9 29.2 %collective-permute-start.9 = (bf16[128,128]{1,0:T(8,128)(2,1)S(1)}, bf16[128,128]{1,0:T(8,128)(2,1)S(1)}, u32[]{:S(2)}, u32[]{:S(2)}) collective-permute-start(bf16[128,128]{1,0:T(8,128)(2,1)S(1)} %get-tuple-element.23), channel_id=1, source_target_pairs={{8,0},{16,8},{24,16},{32,24},{40,32},{48,40},{56,48},{64,56},{72,6... | collective-permute-start | bytes 98312 | tf_op jit(solution)/shard_map/ppermute | solution.py:19
  34.8 20.1 %collective-permute-start.7 = (bf16[128,128]{1,0:T(8,128)(2,1)S(1)}, bf16[128,128]{1,0:T(8,128)(2,1)}, u32[]{:S(2)}, u32[]{:S(2)}) collective-permute-start(bf16[128,128]{1,0:T(8,128)(2,1)S(1)} %get-tuple-element.24), channel_id=1, source_target_pairs={{8,0},{16,8},{24,16},{32,24},{40,32},{48,40},{56,48},{64,56},{72,6... | collective-permute-start | bytes 98312 | tf_op jit(solution)/shard_map/ppermute | solution.py:19
  37.7 8.6 %collective-permute-start.3 = (bf16[128,128]{1,0:T(8,128)(2,1)S(1)}, bf16[128,128]{1,0:T(8,128)(2,1)}, u32[]{:S(2)}, u32[]{:S(2)}) collective-permute-start(bf16[128,128]{1,0:T(8,128)(2,1)S(1)} %get-tuple-element.27), channel_id=1, source_target_pairs={{0,8},{8,16},{16,24},{24,32},{32,40},{40,48},{48,56},{56,64},{64,7... | collective-permute-start | bytes 98312 | tf_op jit(solution)/shard_map/ppermute | solution.py:19
  46.3 13.7 %collective-permute-start.6 = (bf16[128,128]{1,0:T(8,128)(2,1)S(1)}, bf16[128,128]{1,0:T(8,128)(2,1)S(1)}, u32[]{:S(2)}, u32[]{:S(2)}) collective-permute-start(bf16[128,128]{1,0:T(8,128)(2,1)S(1)} %get-tuple-element.25), channel_id=1, source_target_pairs={{1,0},{2,1},{3,2},{4,3},{5,4},{6,5},{7,6},{9,8},{10,9},{11,10},{12... | collective-permute-start | bytes 98312 | tf_op jit(solution)/shard_map/ppermute | solution.py:19
  51.8 8.2 %collective-permute-start.5 = (bf16[128,128]{1,0:T(8,128)(2,1)S(1)}, bf16[128,128]{1,0:T(8,128)(2,1)S(1)}, u32[]{:S(2)}, u32[]{:S(2)}) collective-permute-start(bf16[128,128]{1,0:T(8,128)(2,1)S(1)} %get-tuple-element.26), channel_id=1, source_target_pairs={{0,1},{1,2},{2,3},{3,4},{4,5},{5,6},{6,7},{8,9},{9,10},{10,11},{11... | collective-permute-start | bytes 98312 | tf_op jit(solution)/shard_map/ppermute | solution.py:19
  88.4 143.9 %reduce-scatter.12.cloned.1.call-start = ((), (), s32[]{:S(2)}) async-start(), calls=%async_computation.7 | async-start | bytes 147456
  141.6 13.6 %collective-permute-start.13 = (bf16[128,128]{1,0:T(8,128)(2,1)S(1)}, bf16[128,128]{1,0:T(8,128)(2,1)S(1)}, u32[]{:S(2)}, u32[]{:S(2)}) collective-permute-start(bf16[128,128]{1,0:T(8,128)(2,1)S(1)} %collective-permute-done.12), channel_id=1, source_target_pairs={{0,1},{1,2},{2,3},{3,4},{4,5},{5,6},{6,7},{8,9},{9,10},{10,11},{11... | collective-permute-start | bytes 98312 | tf_op jit(solution)/shard_map/ppermute | solution.py:19
  142.9 21.5 %collective-permute-start.22 = (bf16[128,128]{1,0:T(8,128)(2,1)S(1)}, bf16[128,128]{1,0:T(8,128)(2,1)S(1)}, u32[]{:S(2)}, u32[]{:S(2)}) collective-permute-start(bf16[128,128]{1,0:T(8,128)(2,1)S(1)} %get-tuple-element.14), channel_id=1, source_target_pairs={{8,0},{16,8},{24,16},{32,24},{40,32},{48,40},{56,48},{64,56},{72,6... | collective-permute-start | bytes 98312 | tf_op jit(solution)/shard_map/ppermute | solution.py:19
  146.0 27.4 %collective-permute-start.21 = (bf16[128,128]{1,0:T(8,128)(2,1)S(1)}, bf16[128,128]{1,0:T(8,128)(2,1)S(1)}, u32[]{:S(2)}, u32[]{:S(2)}) collective-permute-start(bf16[128,128]{1,0:T(8,128)(2,1)S(1)} %get-tuple-element.15), channel_id=1, source_target_pairs={{8,0},{16,8},{24,16},{32,24},{40,32},{48,40},{56,48},{64,56},{72,6... | collective-permute-start | bytes 98312 | tf_op jit(solution)/shard_map/ppermute | solution.py:19
  149.3 18.1 %collective-permute-start.19 = (bf16[128,128]{1,0:T(8,128)(2,1)S(1)}, bf16[128,128]{1,0:T(8,128)(2,1)S(1)}, u32[]{:S(2)}, u32[]{:S(2)}) collective-permute-start(bf16[128,128]{1,0:T(8,128)(2,1)S(1)} %get-tuple-element.16), channel_id=1, source_target_pairs={{8,0},{16,8},{24,16},{32,24},{40,32},{48,40},{56,48},{64,56},{72,6... | collective-permute-start | bytes 98312 | tf_op jit(solution)/shard_map/ppermute | solution.py:19
  152.6 8.0 %collective-permute-start.15 = (bf16[128,128]{1,0:T(8,128)(2,1)S(1)}, bf16[128,128]{1,0:T(8,128)(2,1)S(1)}, u32[]{:S(2)}, u32[]{:S(2)}) collective-permute-start(bf16[128,128]{1,0:T(8,128)(2,1)S(1)} %get-tuple-element.19), channel_id=1, source_target_pairs={{0,8},{8,16},{16,24},{24,32},{32,40},{40,48},{48,56},{56,64},{64,7... | collective-permute-start | bytes 98312 | tf_op jit(solution)/shard_map/ppermute | solution.py:19
  160.6 11.9 %collective-permute-start.18 = (bf16[128,128]{1,0:T(8,128)(2,1)S(1)}, bf16[128,128]{1,0:T(8,128)(2,1)S(1)}, u32[]{:S(2)}, u32[]{:S(2)}) collective-permute-start(bf16[128,128]{1,0:T(8,128)(2,1)S(1)} %get-tuple-element.17), channel_id=1, source_target_pairs={{1,0},{2,1},{3,2},{4,3},{5,4},{6,5},{7,6},{9,8},{10,9},{11,10},{12... | collective-permute-start | bytes 98312 | tf_op jit(solution)/shard_map/ppermute | solution.py:19
  164.4 8.1 %collective-permute-start.17 = (bf16[128,128]{1,0:T(8,128)(2,1)S(1)}, bf16[128,128]{1,0:T(8,128)(2,1)S(1)}, u32[]{:S(2)}, u32[]{:S(2)}) collective-permute-start(bf16[128,128]{1,0:T(8,128)(2,1)S(1)} %get-tuple-element.18), channel_id=1, source_target_pairs={{0,1},{1,2},{2,3},{3,4},{4,5},{5,6},{6,7},{8,9},{9,10},{10,11},{11... | collective-permute-start | bytes 98312 | tf_op jit(solution)/shard_map/ppermute | solution.py:19
  200.4 141.3 %reduce-scatter.14.cloned.1.call-start = ((), (), s32[]{:S(2)}) async-start(), calls=%async_computation.8 | async-start | bytes 147456
  250.8 13.6 %collective-permute-start.25 = (bf16[128,128]{1,0:T(8,128)(2,1)S(1)}, bf16[128,128]{1,0:T(8,128)(2,1)S(1)}, u32[]{:S(2)}, u32[]{:S(2)}) collective-permute-start(bf16[128,128]{1,0:T(8,128)(2,1)S(1)} %collective-permute-done.24), channel_id=1, source_target_pairs={{0,1},{1,2},{2,3},{3,4},{4,5},{5,6},{6,7},{8,9},{9,10},{10,11},{11... | collective-permute-start | bytes 98312 | tf_op jit(solution)/shard_map/ppermute | solution.py:19
  252.1 21.5 %collective-permute-start.34 = (bf16[128,128]{1,0:T(8,128)(2,1)S(1)}, bf16[128,128]{1,0:T(8,128)(2,1)S(1)}, u32[]{:S(2)}, u32[]{:S(2)}) collective-permute-start(bf16[128,128]{1,0:T(8,128)(2,1)S(1)} %get-tuple-element.6), channel_id=1, source_target_pairs={{8,0},{16,8},{24,16},{32,24},{40,32},{48,40},{56,48},{64,56},{72,6... | collective-permute-start | bytes 98312 | tf_op jit(solution)/shard_map/ppermute | solution.py:19
  255.3 27.4 %collective-permute-start.33 = (bf16[128,128]{1,0:T(8,128)(2,1)S(1)}, bf16[128,128]{1,0:T(8,128)(2,1)S(1)}, u32[]{:S(2)}, u32[]{:S(2)}) collective-permute-start(bf16[128,128]{1,0:T(8,128)(2,1)S(1)} %get-tuple-element.7), channel_id=1, source_target_pairs={{8,0},{16,8},{24,16},{32,24},{40,32},{48,40},{56,48},{64,56},{72,6... | collective-permute-start | bytes 98312 | tf_op jit(solution)/shard_map/ppermute | solution.py:19
  258.5 18.1 %collective-permute-start.31 = (bf16[128,128]{1,0:T(8,128)(2,1)S(1)}, bf16[128,128]{1,0:T(8,128)(2,1)S(1)}, u32[]{:S(2)}, u32[]{:S(2)}) collective-permute-start(bf16[128,128]{1,0:T(8,128)(2,1)S(1)} %get-tuple-element.8), channel_id=1, source_target_pairs={{8,0},{16,8},{24,16},{32,24},{40,32},{48,40},{56,48},{64,56},{72,6... | collective-permute-start | bytes 98312 | tf_op jit(solution)/shard_map/ppermute | solution.py:19
  269.9 11.9 %collective-permute-start.30 = (bf16[128,128]{1,0:T(8,128)(2,1)S(1)}, bf16[128,128]{1,0:T(8,128)(2,1)S(1)}, u32[]{:S(2)}, u32[]{:S(2)}) collective-permute-start(bf16[128,128]{1,0:T(8,128)(2,1)S(1)} %get-tuple-element.9), channel_id=1, source_target_pairs={{1,0},{2,1},{3,2},{4,3},{5,4},{6,5},{7,6},{9,8},{10,9},{11,10},{12... | collective-permute-start | bytes 98312 | tf_op jit(solution)/shard_map/ppermute | solution.py:19
  273.6 8.2 %collective-permute-start.29 = (bf16[128,128]{1,0:T(8,128)(2,1)S(1)}, bf16[128,128]{1,0:T(8,128)(2,1)S(1)}, u32[]{:S(2)}, u32[]{:S(2)}) collective-permute-start(bf16[128,128]{1,0:T(8,128)(2,1)S(1)} %get-tuple-element.10), channel_id=1, source_target_pairs={{0,1},{1,2},{2,3},{3,4},{4,5},{5,6},{6,7},{8,9},{9,10},{10,11},{11... | collective-permute-start | bytes 98312 | tf_op jit(solution)/shard_map/ppermute | solution.py:19
  (21 other events, 261.7 us)
Sparse Core Ops, SparseCore 0:
  88.5 34.6 reduce-scatter.9
  200.5 31.7 reduce-scatter.11
  309.8 31.8 reduce-scatter.13
